TPU v7x, 32 devices: a whole 2x2x4 slice. The times are simulated.
32 devices in a mesh: groups: 2 (over x), pb: 16 (over z, y, core).
Axes of the slice: x: 2, y: 2, z: 4, core: 2. Of those that a mesh axis runs over, the one named last changes fastest.
Arguments:
- eigvec: bfloat16 [8192, 2592], P(('groups', 'pb')), parts along dimension 0, may hold values from -0.69921875 to 0.69921875
- omega: bfloat16 [8192, 36], P(('groups', 'pb')), parts along dimension 0, may hold values from 0.5 to 4
- phi: bfloat16 [36, 36, 36], replicated, may hold values from -6 to 6
- send_rows: int32 [32, 32], P(('groups', 'pb')), parts along dimension 0, may hold values from 0 to 255
- local_q: int32 [512], P(('groups', 'pb')), parts along dimension 0, may hold values from 0 to 255
- partner_q: int32 [512], P(('groups', 'pb')), parts along dimension 0, may hold values from 0 to 255
- slot_ref: int32 [512], P(('groups', 'pb')), parts along dimension 0, may hold values from 0 to 31, as said below
- tri_count: int32 [32], P(('groups', 'pb')), parts along dimension 0, may hold values from 8 to 16, as said below
Outputs:
- rates: float32 [36, 8192], P(None, ('groups', 'pb')), parts along dimension 1
There are 2 independent parts, one for each index of `groups`. A program takes and returns all parts, laid end to end along the dimension named above; an argument that names none is the same for every part. Nothing has to cross between parts.
Inputs may be any that keep to these rules, and one draw needn't show every extreme that they name: slot_ref of a live triplet of device p names an owner o and a slot s below the number of slots that o fills for p, which is 1 to 2; each device receives 2 filled slots from some owner. `tri_count`: exactly one device has 16 live triplets; live triplets come first.
All inputs are finite; a program needn't handle non-finite values.
Results may differ from a plain program's by a relative error of at most 0.00048.
Values may be sent and summed in bfloat16 or wider, within the bound.
A program may use at most 128 MiB of HBM per device.

v0:
```python
import jax
import jax.numpy as jnp
from jax import lax
from jax.sharding import PartitionSpec as P

NB = 36
BLK = 16
smear_width = 0.5


def triplet_rates(
    phi, near_vec, partner_vec, far_vec, near_freq, partner_freq, far_freq, weight_mask
):
    y_real = jnp.einsum("abc,tnc->tabn", phi, far_vec[:, 0], preferred_element_type=jnp.float32)
    y_imag = -jnp.einsum("abc,tnc->tabn", phi, far_vec[:, 1], preferred_element_type=jnp.float32)
    y_real = y_real.astype(jnp.bfloat16)
    y_imag = y_imag.astype(jnp.bfloat16)
    part_real = partner_vec[:, 0]
    part_imag = partner_vec[:, 1]
    z_real = jnp.einsum(
        "tmb,tabn->tamn", part_real, y_real, preferred_element_type=jnp.float32
    ) - jnp.einsum("tmb,tabn->tamn", part_imag, y_imag, preferred_element_type=jnp.float32)
    z_imag = jnp.einsum(
        "tmb,tabn->tamn", part_real, y_imag, preferred_element_type=jnp.float32
    ) + jnp.einsum("tmb,tabn->tamn", part_imag, y_real, preferred_element_type=jnp.float32)
    z_real = z_real.astype(jnp.bfloat16)
    z_imag = z_imag.astype(jnp.bfloat16)
    near_real = near_vec[:, 0]
    near_imag = near_vec[:, 1]
    v_real = jnp.einsum(
        "tva,tamn->tvmn", near_real, z_real, preferred_element_type=jnp.float32
    ) - jnp.einsum("tva,tamn->tvmn", near_imag, z_imag, preferred_element_type=jnp.float32)
    v_imag = jnp.einsum(
        "tva,tamn->tvmn", near_real, z_imag, preferred_element_type=jnp.float32
    ) + jnp.einsum("tva,tamn->tvmn", near_imag, z_real, preferred_element_type=jnp.float32)
    power = v_real * v_real + v_imag * v_imag
    first = near_freq.astype(jnp.float32)[:, :, None, None]
    second = partner_freq.astype(jnp.float32)[:, None, :, None]
    third = far_freq.astype(jnp.float32)[:, None, None, :]
    offset = (first + second - third) / smear_width
    weight = jnp.exp(-offset * offset) / (first * second * third * NB)
    terms = power * weight * weight_mask[:, None, None, None]
    return (jnp.sum(terms, axis=(2, 3)), jnp.sum(terms, axis=(1, 2)))


def on_device(eigvec, omega, phi, send_rows, local_q, partner_q, slot_ref, tri_count):
    owned = eigvec.shape[0]
    outgoing = send_rows[0]
    sent_vec = jnp.take(eigvec, outgoing, axis=0)
    sent_freq = jnp.take(omega, outgoing, axis=0)
    far_vecs, far_freqs = (
        lax.all_to_all(sent_vec, "pb", split_axis=0, concat_axis=0, tiled=True),
        lax.all_to_all(sent_freq, "pb", split_axis=0, concat_axis=0, tiled=True),
    )
    live = tri_count[0]
    tri_slots = local_q.shape[0]
    empty = jnp.zeros((tri_slots, NB), jnp.float32)

    def one_block(block, carry):
        start = block * BLK
        weight_mask = (start + jnp.arange(BLK, dtype=jnp.int32) < live).astype(jnp.float32)
        near_vec = jnp.take(eigvec, local_q, axis=0).reshape(BLK, 2, NB, NB)
        partner_vec = jnp.take(eigvec, partner_q, axis=0).reshape(BLK, 2, NB, NB)
        far_vec = jnp.take(far_vecs, slot_ref, axis=0).reshape(BLK, 2, NB, NB)
        near_part, far_part = triplet_rates(
            phi,
            near_vec,
            partner_vec,
            far_vec,
            jnp.take(omega, local_q, axis=0),
            jnp.take(omega, partner_q, axis=0),
            jnp.take(far_freqs, slot_ref, axis=0),
            weight_mask,
        )
        return (near_part, far_part)

    upper = (live + BLK - 1) // BLK
    near_terms, far_terms = lax.fori_loop(0, upper, one_block, (empty, empty))
    by_slot = jnp.zeros((NB, outgoing.shape[0]), jnp.float32)
    by_slot = by_slot.at[:, slot_ref].add(far_terms.T)
    returned = lax.all_to_all(by_slot, "pb", split_axis=1, concat_axis=1, tiled=True)
    rates = jnp.zeros((NB, owned), jnp.float32)
    rates = rates.at[:, local_q].add(near_terms.T)
    rates = rates.at[:, outgoing].add(returned)
    return rates


def solution(mesh):
    in_specs = (
        P(("groups", "pb"), None),
        P(("groups", "pb"), None),
        P(),
        P(("groups", "pb"), None),
        P(("groups", "pb")),
        P(("groups", "pb")),
        P(("groups", "pb")),
        P(("groups", "pb")),
    )
    out_specs = P(None, ("groups", "pb"))
    return jax.shard_map(
        on_device, mesh=mesh, in_specs=in_specs, out_specs=out_specs, check_vma=False
    )
```

profile of v0, /device:TPU:0, one launch (start us, length us, event | category | flops | bytes accessed | tf_op | source)
XLA Modules:
  0.0 156.0 jit_solution(6795776041242217636)
XLA Ops:
  0.0 0.7 fusion.20
  0.7 0.5 broadcast.273
  1.2 1.3 reduce.3
  2.6 0.9 copy.32
  3.5 0.6 gather_fusion.2
  4.1 0.7 broadcast_select_fusion.3
  4.7 7.4 %all-to-all-start.1 = ((bf16[16,2,36]{2,1,0:T(2,128)(2,1)}), bf16[16,2,36]{2,1,0:T(2,128)(2,1)S(1)}, u32[]{:S(2)}, u32[]{:S(2)}) async-start(bf16[16,2,36]{2,1,0:T(2,128)(2,1)} %broadcast_select_fusion.3), calls=%async_computation.1 | async-start | bytes 16384 | tf_op jit(solution)/shard_map/all_to_all | solution.py:53
  12.2 0.7 compare_and_fusion.2
  12.8 0.7 compare_select_fusion.5
  13.5 0.7 compare_and_fusion.3
  14.2 0.7 compare_select_fusion.2
  14.8 1.8 %copy.29 = bf16[256,2592]{1,0:T(8,128)(2,1)S(1)} copy(bf16[256,2592]{0,1:T(8,128)(2,1)} %param.14) | data formatting | bytes 2654208 | tf_op args[0]
  16.6 0.7 gather_fusion
  17.3 0.6 gather_fusion.5
  17.9 0.6 gather_fusion.4
  18.6 0.9 broadcast_select_fusion
  19.6 0.7 compare_select_fusion.3
  20.9 0.6 gather_fusion.7
  21.5 0.6 gather_fusion.6
  22.1 6.0 %all-to-all-start = ((bf16[16,2,2592]{2,1,0:T(2,128)(2,1)}), bf16[16,2,2592]{2,1,0:T(2,128)(2,1)S(1)}, u32[]{:S(2)}, u32[]{:S(2)}) async-start(bf16[16,2,2592]{2,1,0:T(2,128)(2,1)} %broadcast_select_fusion), calls=%async_computation | async-start | bytes 344064 | tf_op jit(solution)/shard_map/all_to_all | solution.py:52
  28.2 0.6 gather_fusion.3
  28.8 7.9 %all-to-all-done = bf16[16,2,2592]{2,1,0:T(2,128)(2,1)S(1)} async-done(((bf16[16,2,2592]{2,1,0:T(2,128)(2,1)}), bf16[16,2,2592]{2,1,0:T(2,128)(2,1)S(1)}, u32[]{:S(2)}, u32[]{:S(2)}) %all-to-all-start) | async-done | bytes 165920 | tf_op jit(solution)/shard_map/all_to_all | solution.py:52
  36.8 0.6 gather_fusion.1
  37.4 0.6 broadcast_in_dim.78.clone
  38.0 0.6 broadcast_in_dim.78
  38.6 104.5 %while.15 = (s32[]{:T(128)}, f32[16,36]{1,0:T(8,128)}, f32[16,36]{1,0:T(8,128)}, s32[]{:T(128)}, s32[16]{0:T(128)}, /*index=5*/bf16[16,2592]{1,0:T(8,128)(2,1)S(...) while((s32[]{:T(128)}, f32[16,36]{1,0:T(8,128)}, ...), condition=%wide.region_3.6_spmd, body=%wide.region_0.5_spmd.sunk | while | flops 554730752 | bytes 99940664 | solution.py:78
  38.6 1.3 compare_convert_fusion.2
  40.0 0.4 reshape.252
  40.5 0.4 reshape.251
  41.5 5.2 %fusion.58 = bf16[16,36,36,36]{2,3,1,0:T(8,128)(2,1)} fusion(bf16[36,36,36]{2,1,0:T(8,128)(2,1)} %get-tuple-element.391, bf16[16,2,36,36]{3,2,0,1:T(8,128)(2,1)S(1)} %copy_select_fusion.2), kind=kOutput, calls=%fused_computation.19.clone.1 | convolution fusion | flops 55240704 | bytes 1750144 | tf_op jit(solution)/shard_map/while/body/abc,tnc->tabn/dot_general | solution.py:15
  46.8 2.7 %convolution_convert_fusion.2 = bf16[16,36,36,36]{3,1,2,0:T(8,128)(2,1)S(1)} fusion(bf16[36,36,36]{2,1,0:T(8,128)(2,1)} %get-tuple-element.391, bf16[16,2,36,36]{3,2,0,1:T(8,128)(2,1)S(1)} %copy_select_fusion.2), kind=kOutput, calls=%fused_computation.26.clone.1 | convolution fusion | flops 54494208 | bytes 1750144 | tf_op jit(solution)/shard_map/while/body/abc,tnc->tabn/dot_general | solution.py:14
  49.5 2.5 %copy-done = bf16[16,36,36,36]{3,1,2,0:T(8,128)(2,1)} copy-done((bf16[16,36,36,36]{3,1,2,0:T(8,128)(2,1)}, bf16[16,36,36,36]{3,1,2,0:T(8,128)(2,1)S(1)}, u32[]{:S(2)}) %copy-start) | copy-done | bytes 1493016 | tf_op jit(solution)/shard_map/while
  52.0 5.3 %fusion.61 = f32[16,36,36,36]{3,2,1,0:T(8,128)} fusion(bf16[16,36,36,36]{3,1,2,0:T(8,128)(2,1)S(1)} %convolution_convert_fusion.2, bf16[16,2,36,36]{3,2,1,0:T(8,128)(2,1)S(1)} %reshape.251), kind=kOutput, calls=%fused_computation.24.clone.1 | convolution fusion | flops 53747712 | bytes 9048064 | tf_op jit(solution)/shard_map/while/body/tmb,tabn->tamn/dot_general | solution.py:20
  57.3 10.2 %fusion.62 = bf16[16,36,36,36]{2,3,1,0:T(8,128)(2,1)} fusion(f32[16,36,36,36]{3,2,1,0:T(8,128)} %fusion.61, bf16[16,36,36,36]{2,3,1,0:T(8,128)(2,1)} %fusion.58, bf16[16,2,36,36]{3,2,1,0:T(8,128)(2,1)S(1)} %reshape.251), kind=kOutput, calls=%fused_computation.20.clone.1 | convolution fusion | flops 55240704 | bytes 6135808 | tf_op jit(solution)/shard_map/while/body/tmb,tabn->tamn/dot_general | solution.py:22
  67.5 9.9 %copy.52 = bf16[16,36,36,36]{1,3,2,0:T(8,128)(2,1)} copy(bf16[16,36,36,36]{2,3,1,0:T(8,128)(2,1)} %fusion.62) | data formatting | bytes 2985984 | tf_op jit(solution)/shard_map/while/body/convert_element_type | solution.py:26
  77.4 8.7 %fusion.57 = f32[16,36,36,36]{3,2,1,0:T(8,128)} fusion(bf16[16,36,36,36]{3,1,2,0:T(8,128)(2,1)} %copy-done, bf16[16,2,36,36]{3,2,1,0:T(8,128)(2,1)S(1)} %reshape.251), kind=kOutput, calls=%fused_computation.22.clone.1 | convolution fusion | flops 53747712 | bytes 4642816 | tf_op jit(solution)/shard_map/while/body/tmb,tabn->tamn/dot_general | solution.py:25
  86.1 10.3 %fusion.59 = bf16[16,36,36,36]{2,3,1,0:T(8,128)(2,1)} fusion(f32[16,36,36,36]{3,2,1,0:T(8,128)} %fusion.57, bf16[16,36,36,36]{2,3,1,0:T(8,128)(2,1)} %fusion.58, bf16[16,2,36,36]{3,2,1,0:T(8,128)(2,1)S(1)} %reshape.251), kind=kOutput, calls=%fused_computation.21.clone.1 | convolution fusion | flops 55240704 | bytes 6135808 | tf_op jit(solution)/shard_map/while/body/tmb,tabn->tamn/dot_general | solution.py:23
  96.4 9.9 %copy.51 = bf16[16,36,36,36]{1,3,2,0:T(8,128)(2,1)} copy(bf16[16,36,36,36]{2,3,1,0:T(8,128)(2,1)} %fusion.59) | data formatting | bytes 2985984 | tf_op jit(solution)/shard_map/while/body/convert_element_type | solution.py:27
  106.2 8.9 %fusion.64 = f32[16,36,36,36]{3,2,1,0:T(8,128)} fusion(bf16[16,36,36,36]{1,3,2,0:T(8,128)(2,1)} %copy.51, bf16[16,2,36,36]{3,2,1,0:T(8,128)(2,1)S(1)} %reshape.252), kind=kOutput, calls=%fused_computation.40.clone.1 | convolution fusion | flops 53747712 | bytes 4642816 | tf_op jit(solution)/shard_map/while/body/tva,tamn->tvmn/dot_general | solution.py:32
  115.1 5.2 %fusion.60 = f32[16,36,36,36]{3,2,1,0:T(8,128)} fusion(bf16[16,36,36,36]{1,3,2,0:T(8,128)(2,1)S(1)} %copy-done.1, bf16[16,2,36,36]{3,2,1,0:T(8,128)(2,1)S(1)} %reshape.252), kind=kOutput, calls=%fused_computation.38.clone.1 | convolution fusion | flops 53747712 | bytes 9048064 | tf_op jit(solution)/shard_map/while/body/tva,tamn->tvmn/dot_general | solution.py:33
  120.3 5.2 %fusion.63 = f32[16,36,36,36]{3,2,1,0:T(8,128)} fusion(bf16[16,36,36,36]{1,3,2,0:T(8,128)(2,1)S(1)} %bitcast.133, bf16[16,2,36,36]{3,2,1,0:T(8,128)(2,1)S(1)} %reshape.252), kind=kOutput, calls=%fused_computation.39.clone.1 | convolution fusion | flops 53747712 | bytes 9048064 | tf_op jit(solution)/shard_map/while/body/tva,tamn->tvmn/dot_general | solution.py:30
  125.5 17.6 %fusion.65 = (f32[16,36]{1,0:T(8,128)}, f32[16,36]{1,0:T(8,128)}) fusion(f32[16]{0:T(128)S(1)} %get-tuple-element.349, f32[16,36,36]{1,2,0:T(8,128)S(1)} %get-tuple-element.350, f32[16,36]{1,0:T(8,128)S(1)} %select_convert_fusion.2, f32[16,36,36]{1,2,0:T(8,128)S(1)} %get-tuple-element.352, f32[16,36,36,36]{3,2,1,0:T(8,128)} %fusion.60, ...), kind=kOutput, calls=%fused_computation.68.clone.1 | convolution fusion | flops 65690496 | bytes 11283456 | tf_op jit(solution)/shard_map/while/body/tva,tamn->tvmn/dot_general | solution.py:35
  143.2 1.4 scatter_custom_fusion.1
  144.5 3.5 %all-to-all-start.2 = ((f32[36,16,2]{0,2,1:T(2,128)}), f32[36,16,2]{0,2,1:T(2,128)S(1)}, u32[]{:S(2)}, u32[]{:S(2)}) async-start(f32[36,16,2]{0,2,1:T(2,128)} %bitcast.33), calls=%async_computation.2 | async-start | bytes 32768 | tf_op jit(solution)/shard_map/all_to_all | solution.py:81
  148.0 0.9 scatter_custom_fusion
  148.9 5.6 %all-to-all-done.2 = f32[36,16,2]{0,2,1:T(2,128)S(1)} async-done(((f32[36,16,2]{0,2,1:T(2,128)}), f32[36,16,2]{0,2,1:T(2,128)S(1)}, u32[]{:S(2)}, u32[]{:S(2)}) %all-to-all-start.2) | async-done | bytes 4640 | tf_op jit(solution)/shard_map/all_to_all | solution.py:81
  154.5 0.8 scatter_fusion
  155.3 0.7 copy.35
  (33 shorter events, 1.2 us)
Async XLA Ops:
  0.7 1.8 %copy-start.2 = (s32[32]{0:T(128)}, s32[32]{0:T(128)S(1)}, u32[]{:S(2)}) copy-start(s32[32]{0:T(128)S(1)} %fusion.20) | copy-start | bytes 388
  4.7 17.4 %all-to-all-start.1 = ((bf16[16,2,36]{2,1,0:T(2,128)(2,1)}), bf16[16,2,36]{2,1,0:T(2,128)(2,1)S(1)}, u32[]{:S(2)}, u32[]{:S(2)}) async-start(bf16[16,2,36]{2,1,0:T(2,128)(2,1)} %broadcast_select_fusion.3), calls=%async_computation.1 | async-start | bytes 16384 | tf_op jit(solution)/shard_map/all_to_all | solution.py:53
  13.5 3.1 %copy-start.4 = (s32[16]{0:T(128)}, s32[16]{0:T(128)S(1)}, u32[]{:S(2)}) copy-start(s32[16]{0:T(128)S(1)} %compare_select_fusion.5) | copy-start | bytes 196
  20.3 18.4 %copy-start.5 = (s32[16]{0:T(128)}, s32[16]{0:T(128)S(1)}, u32[]{:S(2)}) copy-start(s32[16]{0:T(128)S(1)} %compare_select_fusion.3) | copy-start | bytes 196
  22.1 14.6 %all-to-all-start = ((bf16[16,2,2592]{2,1,0:T(2,128)(2,1)}), bf16[16,2,2592]{2,1,0:T(2,128)(2,1)S(1)}, u32[]{:S(2)}, u32[]{:S(2)}) async-start(bf16[16,2,2592]{2,1,0:T(2,128)(2,1)} %broadcast_select_fusion), calls=%async_computation | async-start | bytes 344064 | tf_op jit(solution)/shard_map/all_to_all | solution.py:52
  38.6 115.9 %copy-start.3 = (s32[32]{0:T(128)S(1)}, s32[32]{0:T(128)}, u32[]{:S(2)}) copy-start(s32[32]{0:T(128)} %copy-done.2) | copy-start | bytes 388
  49.5 2.5 %copy-start = (bf16[16,36,36,36]{3,1,2,0:T(8,128)(2,1)}, bf16[16,36,36,36]{3,1,2,0:T(8,128)(2,1)S(1)}, u32[]{:S(2)}) copy-start(bf16[16,36,36,36]{3,1,2,0:T(8,128)(2,1)S(1)} %convolution_convert_fusion.2) | copy-start | bytes 4478980 | tf_op jit(solution)/shard_map/while
  106.2 8.9 %copy-start.1 = (bf16[16,36,36,36]{1,3,2,0:T(8,128)(2,1)S(1)}, bf16[16,36,36,36]{1,3,2,0:T(8,128)(2,1)}, u32[]{:S(2)}) copy-start(bf16[16,36,36,36]{1,3,2,0:T(8,128)(2,1)} %copy.51) | copy-start | bytes 4478980 | tf_op jit(solution)/shard_map/while
  106.2 14.1 %slice-start = ((s8[5898240]{0:T(1024)(128)(4,1)}), s8[4194304]{0:T(1024)(128)(4,1)S(1)}, s32[]{:S(2)}) async-start(s8[5898240]{0:T(1024)(128)(4,1)} %bitcast.132), calls=%async_computation.3 | async-start | bytes 8388608 | tf_op jit(solution)/shard_map/while
  115.1 5.2 %slice-start.1 = ((s8[5898240]{0:T(1024)(128)(4,1)}), s8[1703936]{0:T(1024)(128)(4,1)S(1)}, s32[]{:S(2)}) async-start(s8[5898240]{0:T(1024)(128)(4,1)} %bitcast.132), calls=%async_computation.4 | async-start | bytes 3407872 | tf_op jit(solution)/shard_map/while
  144.5 10.0 %all-to-all-start.2 = ((f32[36,16,2]{0,2,1:T(2,128)}), f32[36,16,2]{0,2,1:T(2,128)S(1)}, u32[]{:S(2)}, u32[]{:S(2)}) async-start(f32[36,16,2]{0,2,1:T(2,128)} %bitcast.33), calls=%async_computation.2 | async-start | bytes 32768 | tf_op jit(solution)/shard_map/all_to_all | solution.py:81
where the time goes:
time: 157 us; the launch traced here: 156 us
  matrix products  79.3 us (51%)
  local copies, waits for them, and re-layouts  33.6 us (21%)
  starting transfers between devices  16.9 us (11%)
  waiting for transfers between devices  13.5 us (9%)
  other arithmetic  11.7 us (7%)
    dot_general x1, matrix products, triplet_rates(): jnp.einsum('tva,tamn->tvmn', near_imag, z_real, preferred_element_type=jn...  17.6 us
    dot_general x1, matrix products, triplet_rates(): jnp.einsum('tmb,tabn->tamn', part_real, y_imag, preferred_element_type=jn...  10.3 us
    dot_general x1, matrix products, triplet_rates(): jnp.einsum('tmb,tabn->tamn', part_imag, y_imag, preferred_element_type=jn...  10.2 us
    convert_element_type x1, local copies, waits for them, and re-layouts, triplet_rates(): z_imag = z_imag.astype(jnp.bfloat16)  9.87 us
    convert_element_type x1, local copies, waits for them, and re-layouts, triplet_rates(): z_real = z_real.astype(jnp.bfloat16)  9.85 us
    dot_general x1, matrix products, triplet_rates(): jnp.einsum('tva,tamn->tvmn', near_imag, z_imag, preferred_element_type=jn...  8.89 us
    dot_general x1, matrix products, triplet_rates(): jnp.einsum('tmb,tabn->tamn', part_imag, y_real, preferred_element_type=jn...  8.74 us
    all_to_all x1, waiting for transfers between devices, on_device(): lax.all_to_all(sent_vec, 'pb', split_axis=0, concat_axis=0, tiled=True)  7.9 us
  transfers between devices with their start and end apart: 3, of which 2 were waited for; matrix products, arithmetic and copies ran while one was open for 7% of the time, Pallas kernels for 0%

commit v1 on v0

--- a/solution.py
+++ b/solution.py
@@ -78,7 +78,9 @@
     near_terms, far_terms = lax.fori_loop(0, upper, one_block, (empty, empty))
     by_slot = jnp.zeros((NB, outgoing.shape[0]), jnp.float32)
     by_slot = by_slot.at[:, slot_ref].add(far_terms.T)
-    returned = lax.all_to_all(by_slot, "pb", split_axis=1, concat_axis=1, tiled=True)
+    parts = jnp.split(by_slot, lax.axis_size("pb"), axis=1)
+    received = lax.all_to_all(jnp.stack(parts), "pb", 0, 0)
+    returned = jnp.concatenate(received, axis=1)
     rates = jnp.zeros((NB, owned), jnp.float32)
     rates = rates.at[:, local_q].add(near_terms.T)
     rates = rates.at[:, outgoing].add(returned)

time: 157 us -> 166 us (1.057)
  local copies, waits for them, and re-layouts: 33.6 us -> 42.7 us
    unnamed x11 -> x26, local copies, waits for them, and re-layouts: 3.18 us -> 11.6 us
where the time goes in v1:
time: 166 us; the launch traced here: 165 us
  matrix products  79.3 us (48%)
  local copies, waits for them, and re-layouts  42.7 us (26%)
  starting transfers between devices  16.9 us (10%)
  waiting for transfers between devices  13.5 us (8%)
  other arithmetic  11.3 us (7%)
    dot_general x1, matrix products, triplet_rates(): jnp.einsum('tva,tamn->tvmn', near_imag, z_real, preferred_element_type=jn...  17.6 us
    unnamed x26, local copies, waits for them, and re-layouts  11.6 us
    dot_general x1, matrix products, triplet_rates(): jnp.einsum('tmb,tabn->tamn', part_real, y_imag, preferred_element_type=jn...  10.3 us
    dot_general x1, matrix products, triplet_rates(): jnp.einsum('tmb,tabn->tamn', part_imag, y_imag, preferred_element_type=jn...  10.2 us
    convert_element_type x1, local copies, waits for them, and re-layouts, triplet_rates(): z_imag = z_imag.astype(jnp.bfloat16)  9.88 us
    convert_element_type x1, local copies, waits for them, and re-layouts, triplet_rates(): z_real = z_real.astype(jnp.bfloat16)  9.84 us
    dot_general x1, matrix products, triplet_rates(): jnp.einsum('tva,tamn->tvmn', near_imag, z_imag, preferred_element_type=jn...  8.89 us
    dot_general x1, matrix products, triplet_rates(): jnp.einsum('tmb,tabn->tamn', part_imag, y_real, preferred_element_type=jn...  8.74 us
  transfers between devices with their start and end apart: 3, of which 2 were waited for; matrix products, arithmetic and copies ran while one was open for 7% of the time, Pallas kernels for 0%

profile of v1, /device:TPU:0, one launch (start us, length us, event | category | flops | bytes accessed | tf_op | source)
XLA Modules:
  0.0 164.6 jit_solution(12559125890154862435)
XLA Ops:
  0.0 0.7 fusion.20
  1.2 1.3 reduce.3
  2.6 0.9 copy.32
  3.5 0.6 gather_fusion.2
  4.1 0.7 broadcast_select_fusion.3
  4.7 7.4 %all-to-all-start.1 = ((bf16[16,2,36]{2,1,0:T(2,128)(2,1)}), bf16[16,2,36]{2,1,0:T(2,128)(2,1)S(1)}, u32[]{:S(2)}, u32[]{:S(2)}) async-start(bf16[16,2,36]{2,1,0:T(2,128)(2,1)} %broadcast_select_fusion.3), calls=%async_computation.1 | async-start | bytes 16384 | tf_op jit(solution)/shard_map/all_to_all | solution.py:53
  12.2 0.7 compare_and_fusion.2
  12.8 0.7 compare_select_fusion.5
  13.5 0.7 compare_and_fusion.3
  14.2 0.7 compare_select_fusion.2
  14.8 0.6 gather_fusion.7
  15.4 1.8 %copy.29 = bf16[256,2592]{1,0:T(8,128)(2,1)S(1)} copy(bf16[256,2592]{0,1:T(8,128)(2,1)} %param.14) | data formatting | bytes 2654208 | tf_op args[0]
  17.2 0.6 gather_fusion.4
  17.8 0.7 gather_fusion
  18.5 0.6 gather_fusion.5
  19.3 0.9 broadcast_select_fusion
  20.3 0.7 compare_select_fusion.3
  21.6 0.6 gather_fusion.6
  22.2 6.0 %all-to-all-start = ((bf16[16,2,2592]{2,1,0:T(2,128)(2,1)}), bf16[16,2,2592]{2,1,0:T(2,128)(2,1)S(1)}, u32[]{:S(2)}, u32[]{:S(2)}) async-start(bf16[16,2,2592]{2,1,0:T(2,128)(2,1)} %broadcast_select_fusion), calls=%async_computation | async-start | bytes 344064 | tf_op jit(solution)/shard_map/all_to_all | solution.py:52
  28.4 0.6 gather_fusion.3
  28.9 7.9 %all-to-all-done = bf16[16,2,2592]{2,1,0:T(2,128)(2,1)S(1)} async-done(((bf16[16,2,2592]{2,1,0:T(2,128)(2,1)}), bf16[16,2,2592]{2,1,0:T(2,128)(2,1)S(1)}, u32[]{:S(2)}, u32[]{:S(2)}) %all-to-all-start) | async-done | bytes 165920 | tf_op jit(solution)/shard_map/all_to_all | solution.py:52
  37.0 0.6 gather_fusion.1
  37.6 0.6 broadcast_in_dim.78.clone
  38.2 0.6 broadcast_in_dim.78
  38.8 104.5 %while.15 = (s32[]{:T(128)}, f32[16,36]{1,0:T(8,128)}, f32[16,36]{1,0:T(8,128)}, s32[]{:T(128)}, s32[16]{0:T(128)}, /*index=5*/bf16[16,2592]{1,0:T(8,128)(2,1)S(...) while((s32[]{:T(128)}, f32[16,36]{1,0:T(8,128)}, ...), condition=%wide.region_3.6_spmd, body=%wide.region_0.5_spmd.sunk | while | flops 554730752 | bytes 99940664 | solution.py:78
  38.8 1.3 compare_convert_fusion.2
  41.7 5.2 %fusion.58 = bf16[16,36,36,36]{2,3,1,0:T(8,128)(2,1)} fusion(bf16[36,36,36]{2,1,0:T(8,128)(2,1)} %get-tuple-element.389, bf16[16,2,36,36]{3,2,0,1:T(8,128)(2,1)S(1)} %copy_select_fusion.2), kind=kOutput, calls=%fused_computation.19.clone.1 | convolution fusion | flops 55240704 | bytes 1750144 | tf_op jit(solution)/shard_map/while/body/abc,tnc->tabn/dot_general | solution.py:15
  46.9 2.7 %convolution_convert_fusion.2 = bf16[16,36,36,36]{3,1,2,0:T(8,128)(2,1)S(1)} fusion(bf16[36,36,36]{2,1,0:T(8,128)(2,1)} %get-tuple-element.389, bf16[16,2,36,36]{3,2,0,1:T(8,128)(2,1)S(1)} %copy_select_fusion.2), kind=kOutput, calls=%fused_computation.26.clone.1 | convolution fusion | flops 54494208 | bytes 1750144 | tf_op jit(solution)/shard_map/while/body/abc,tnc->tabn/dot_general | solution.py:14
  49.6 2.5 %copy-done = bf16[16,36,36,36]{3,1,2,0:T(8,128)(2,1)} copy-done((bf16[16,36,36,36]{3,1,2,0:T(8,128)(2,1)}, bf16[16,36,36,36]{3,1,2,0:T(8,128)(2,1)S(1)}, u32[]{:S(2)}) %copy-start) | copy-done | bytes 1493016 | tf_op jit(solution)/shard_map/while
  52.1 5.3 %fusion.61 = f32[16,36,36,36]{3,2,1,0:T(8,128)} fusion(bf16[16,36,36,36]{3,1,2,0:T(8,128)(2,1)S(1)} %convolution_convert_fusion.2, bf16[16,2,36,36]{3,2,1,0:T(8,128)(2,1)S(1)} %reshape.257), kind=kOutput, calls=%fused_computation.24.clone.1 | convolution fusion | flops 53747712 | bytes 9048064 | tf_op jit(solution)/shard_map/while/body/tmb,tabn->tamn/dot_general | solution.py:20
  57.4 10.2 %fusion.62 = bf16[16,36,36,36]{2,3,1,0:T(8,128)(2,1)} fusion(f32[16,36,36,36]{3,2,1,0:T(8,128)} %fusion.61, bf16[16,36,36,36]{2,3,1,0:T(8,128)(2,1)} %fusion.58, bf16[16,2,36,36]{3,2,1,0:T(8,128)(2,1)S(1)} %reshape.257), kind=kOutput, calls=%fused_computation.20.clone.1 | convolution fusion | flops 55240704 | bytes 6135808 | tf_op jit(solution)/shard_map/while/body/tmb,tabn->tamn/dot_general | solution.py:22
  67.7 9.8 %copy.52 = bf16[16,36,36,36]{1,3,2,0:T(8,128)(2,1)} copy(bf16[16,36,36,36]{2,3,1,0:T(8,128)(2,1)} %fusion.62) | data formatting | bytes 2985984 | tf_op jit(solution)/shard_map/while/body/convert_element_type | solution.py:26
  77.5 8.7 %fusion.57 = f32[16,36,36,36]{3,2,1,0:T(8,128)} fusion(bf16[16,36,36,36]{3,1,2,0:T(8,128)(2,1)} %copy-done, bf16[16,2,36,36]{3,2,1,0:T(8,128)(2,1)S(1)} %reshape.257), kind=kOutput, calls=%fused_computation.22.clone.1 | convolution fusion | flops 53747712 | bytes 4642816 | tf_op jit(solution)/shard_map/while/body/tmb,tabn->tamn/dot_general | solution.py:25
  86.2 10.3 %fusion.59 = bf16[16,36,36,36]{2,3,1,0:T(8,128)(2,1)} fusion(f32[16,36,36,36]{3,2,1,0:T(8,128)} %fusion.57, bf16[16,36,36,36]{2,3,1,0:T(8,128)(2,1)} %fusion.58, bf16[16,2,36,36]{3,2,1,0:T(8,128)(2,1)S(1)} %reshape.257), kind=kOutput, calls=%fused_computation.21.clone.1 | convolution fusion | flops 55240704 | bytes 6135808 | tf_op jit(solution)/shard_map/while/body/tmb,tabn->tamn/dot_general | solution.py:23
  96.5 9.9 %copy.51 = bf16[16,36,36,36]{1,3,2,0:T(8,128)(2,1)} copy(bf16[16,36,36,36]{2,3,1,0:T(8,128)(2,1)} %fusion.59) | data formatting | bytes 2985984 | tf_op jit(solution)/shard_map/while/body/convert_element_type | solution.py:27
  106.4 8.9 %fusion.64 = f32[16,36,36,36]{3,2,1,0:T(8,128)} fusion(bf16[16,36,36,36]{1,3,2,0:T(8,128)(2,1)} %copy.51, bf16[16,2,36,36]{3,2,1,0:T(8,128)(2,1)S(1)} %reshape.258), kind=kOutput, calls=%fused_computation.40.clone.1 | convolution fusion | flops 53747712 | bytes 4642816 | tf_op jit(solution)/shard_map/while/body/tva,tamn->tvmn/dot_general | solution.py:32
  115.3 5.2 %fusion.60 = f32[16,36,36,36]{3,2,1,0:T(8,128)} fusion(bf16[16,36,36,36]{1,3,2,0:T(8,128)(2,1)S(1)} %copy-done.1, bf16[16,2,36,36]{3,2,1,0:T(8,128)(2,1)S(1)} %reshape.258), kind=kOutput, calls=%fused_computation.38.clone.1 | convolution fusion | flops 53747712 | bytes 9048064 | tf_op jit(solution)/shard_map/while/body/tva,tamn->tvmn/dot_general | solution.py:33
  120.5 5.2 %fusion.63 = f32[16,36,36,36]{3,2,1,0:T(8,128)} fusion(bf16[16,36,36,36]{1,3,2,0:T(8,128)(2,1)S(1)} %bitcast.198, bf16[16,2,36,36]{3,2,1,0:T(8,128)(2,1)S(1)} %reshape.258), kind=kOutput, calls=%fused_computation.39.clone.1 | convolution fusion | flops 53747712 | bytes 9048064 | tf_op jit(solution)/shard_map/while/body/tva,tamn->tvmn/dot_general | solution.py:30
  125.6 17.6 %fusion.65 = (f32[16,36]{1,0:T(8,128)}, f32[16,36]{1,0:T(8,128)}) fusion(f32[16]{0:T(128)S(1)} %get-tuple-element.347, f32[16,36,36]{1,2,0:T(8,128)S(1)} %get-tuple-element.348, f32[16,36]{1,0:T(8,128)S(1)} %select_convert_fusion.2, f32[16,36,36]{1,2,0:T(8,128)S(1)} %get-tuple-element.350, f32[16,36,36,36]{3,2,1,0:T(8,128)} %fusion.60, ...), kind=kOutput, calls=%fused_computation.100.clone.1 | convolution fusion | flops 65690496 | bytes 11283456 | tf_op jit(solution)/shard_map/while/body/tva,tamn->tvmn/dot_general | solution.py:35
  143.3 0.8 scatter_custom_fusion.1
  144.1 0.6 constant_dynamic-update-slice_fusion.15
  145.8 0.6 constant_dynamic-update-slice_fusion.12
  146.9 0.6 constant_dynamic-update-slice_fusion.10
  153.1 3.5 %all-to-all-start.2 = ((f32[16,36,2]{1,2,0:T(2,128)}), f32[16,36,2]{1,2,0:T(2,128)S(1)}, u32[]{:S(2)}, u32[]{:S(2)}) async-start(f32[16,36,2]{1,2,0:T(2,128)} %constant_dynamic-update-slice_fusion), calls=%async_computation.2 | async-start | bytes 32768 | tf_op jit(solution)/shard_map/all_to_all | solution.py:82
  156.6 0.9 scatter_custom_fusion
  157.5 5.6 %all-to-all-done.2 = f32[16,36,2]{1,2,0:T(2,128)S(1)} async-done(((f32[16,36,2]{1,2,0:T(2,128)}), f32[16,36,2]{1,2,0:T(2,128)S(1)}, u32[]{:S(2)}, u32[]{:S(2)}) %all-to-all-start.2) | async-done | bytes 4640 | tf_op jit(solution)/shard_map/all_to_all | solution.py:82
  163.1 0.8 scatter_fusion
  163.9 0.7 copy.35
  (50 shorter events, 10.0 us)
Async XLA Ops:
  0.7 1.8 %copy-start.2 = (s32[32]{0:T(128)}, s32[32]{0:T(128)S(1)}, u32[]{:S(2)}) copy-start(s32[32]{0:T(128)S(1)} %fusion.20) | copy-start | bytes 388
  4.7 17.5 %all-to-all-start.1 = ((bf16[16,2,36]{2,1,0:T(2,128)(2,1)}), bf16[16,2,36]{2,1,0:T(2,128)(2,1)S(1)}, u32[]{:S(2)}, u32[]{:S(2)}) async-start(bf16[16,2,36]{2,1,0:T(2,128)(2,1)} %broadcast_select_fusion.3), calls=%async_computation.1 | async-start | bytes 16384 | tf_op jit(solution)/shard_map/all_to_all | solution.py:53
  13.5 5.0 %copy-start.4 = (s32[16]{0:T(128)}, s32[16]{0:T(128)S(1)}, u32[]{:S(2)}) copy-start(s32[16]{0:T(128)S(1)} %compare_select_fusion.5) | copy-start | bytes 196
  21.0 17.8 %copy-start.5 = (s32[16]{0:T(128)}, s32[16]{0:T(128)S(1)}, u32[]{:S(2)}) copy-start(s32[16]{0:T(128)S(1)} %compare_select_fusion.3) | copy-start | bytes 196
  22.2 14.6 %all-to-all-start = ((bf16[16,2,2592]{2,1,0:T(2,128)(2,1)}), bf16[16,2,2592]{2,1,0:T(2,128)(2,1)S(1)}, u32[]{:S(2)}, u32[]{:S(2)}) async-start(bf16[16,2,2592]{2,1,0:T(2,128)(2,1)} %broadcast_select_fusion), calls=%async_computation | async-start | bytes 344064 | tf_op jit(solution)/shard_map/all_to_all | solution.py:52
  38.8 124.3 %copy-start.3 = (s32[32]{0:T(128)S(1)}, s32[32]{0:T(128)}, u32[]{:S(2)}) copy-start(s32[32]{0:T(128)} %copy-done.2) | copy-start | bytes 388
  49.6 2.5 %copy-start = (bf16[16,36,36,36]{3,1,2,0:T(8,128)(2,1)}, bf16[16,36,36,36]{3,1,2,0:T(8,128)(2,1)S(1)}, u32[]{:S(2)}) copy-start(bf16[16,36,36,36]{3,1,2,0:T(8,128)(2,1)S(1)} %convolution_convert_fusion.2) | copy-start | bytes 4478980 | tf_op jit(solution)/shard_map/while
  106.4 8.9 %copy-start.1 = (bf16[16,36,36,36]{1,3,2,0:T(8,128)(2,1)S(1)}, bf16[16,36,36,36]{1,3,2,0:T(8,128)(2,1)}, u32[]{:S(2)}) copy-start(bf16[16,36,36,36]{1,3,2,0:T(8,128)(2,1)} %copy.51) | copy-start | bytes 4478980 | tf_op jit(solution)/shard_map/while
  106.4 14.1 %slice-start = ((s8[5898240]{0:T(1024)(128)(4,1)}), s8[4194304]{0:T(1024)(128)(4,1)S(1)}, s32[]{:S(2)}) async-start(s8[5898240]{0:T(1024)(128)(4,1)} %bitcast.197), calls=%async_computation.3 | async-start | bytes 8388608 | tf_op jit(solution)/shard_map/while
  115.3 5.2 %slice-start.1 = ((s8[5898240]{0:T(1024)(128)(4,1)}), s8[1703936]{0:T(1024)(128)(4,1)S(1)}, s32[]{:S(2)}) async-start(s8[5898240]{0:T(1024)(128)(4,1)} %bitcast.197), calls=%async_computation.4 | async-start | bytes 3407872 | tf_op jit(solution)/shard_map/while
  153.1 10.0 %all-to-all-start.2 = ((f32[16,36,2]{1,2,0:T(2,128)}), f32[16,36,2]{1,2,0:T(2,128)S(1)}, u32[]{:S(2)}, u32[]{:S(2)}) async-start(f32[16,36,2]{1,2,0:T(2,128)} %constant_dynamic-update-slice_fusion), calls=%async_computation.2 | async-start | bytes 32768 | tf_op jit(solution)/shard_map/all_to_all | solution.py:82
